TPU v7x, 32 devices: a whole 2x2x4 slice. The times are simulated.
32 devices in a mesh: gx: 4 (over y, x), gy: 2 (over core), gz: 4 (over z).
Axes of the slice: x: 2, y: 2, z: 4, core: 2. Of those that a mesh axis runs over, the one named last changes fastest.
Arguments:
- tokens: bfloat16 [192, 12288], P(('gy', 'gz'), 'gx'), may hold values from -6 to 6
- grad_out: bfloat16 [192, 12288], P(('gy', 'gz'), 'gx'), may hold values from -0.86328125 to 0.86328125
- w_in: bfloat16 [12288, 24576], P('gx', ('gy', 'gz')), may hold values from -0.0546875 to 0.0546875
- w_out: bfloat16 [24576, 12288], P(('gy', 'gz'), 'gx'), may hold values from -0.0390625 to 0.0390625
Outputs:
- output: float32 [192, 12288], P(('gy', 'gz'), 'gx')
- grad_in: float32 [192, 12288], P(('gy', 'gz'), 'gx')
- grad_w_in: bfloat16 [12288, 24576], P('gx', ('gy', 'gz'))
- grad_w_out: bfloat16 [24576, 12288], P(('gy', 'gz'), 'gx')
All inputs are finite; a program needn't handle non-finite values.
Results may differ from a plain program's by a relative error of at most 0.0049.
Values may be sent and summed in bfloat16 or wider, within the bound.
A program may use at most 128 MiB of HBM per device.

v0:
```python
import jax
import jax.numpy as jnp
from jax import lax
from jax.sharding import PartitionSpec as P


def activate(pre_sum, back_sum):
    scale_c = 0.7978845608
    inner_arg = scale_c * (pre_sum + 0.044715 * pre_sum * pre_sum * pre_sum)
    tanh_val = jnp.tanh(inner_arg)
    value = 0.5 * pre_sum * (1.0 + tanh_val)
    deriv = 0.5 * (1.0 + tanh_val) + 0.5 * pre_sum * (1.0 - tanh_val * tanh_val) * scale_c * (
        1.0 + 3.0 * 0.044715 * pre_sum * pre_sum
    )
    return (value.astype(jnp.bfloat16), (back_sum * deriv).astype(jnp.bfloat16))


def right_product(left, right):
    return lax.dot_general(
        left, right, (((1,), (1,)), ((), ())), preferred_element_type=jnp.float32
    )


def left_product(left, right):
    return lax.dot_general(
        left, right, (((0,), (0,)), ((), ())), preferred_element_type=jnp.float32
    )


def shards(tokens, grad_out, w_in, w_out):
    token_rows, grad_rows = (
        lax.all_gather(tokens, ("gy", "gz"), axis=0, tiled=True),
        lax.all_gather(grad_out, ("gy", "gz"), axis=0, tiled=True),
    )
    pre_part = jnp.dot(token_rows, w_in, preferred_element_type=jnp.float32)
    back_part = right_product(grad_rows, w_out)
    pre_sum, back_sum = lax.psum((pre_part, back_part), "gx")
    hidden, slopes = activate(pre_sum, back_sum)
    picked = hidden
    output = lax.psum_scatter(
        jnp.dot(picked, w_out, preferred_element_type=jnp.float32),
        ("gy", "gz"),
        scatter_dimension=0,
        tiled=True,
    )
    picked = slopes
    grad_in = lax.psum_scatter(
        right_product(picked, w_in), ("gy", "gz"), scatter_dimension=0, tiled=True
    )
    grad_w_in = left_product(token_rows, slopes).astype(jnp.bfloat16)
    grad_w_out = left_product(hidden, grad_rows).astype(jnp.bfloat16)
    return (output, grad_in, grad_w_in, grad_w_out)


def solution(mesh):
    placed = (
        P(("gy", "gz"), "gx"),
        P(("gy", "gz"), "gx"),
        P("gx", ("gy", "gz")),
        P(("gy", "gz"), "gx"),
    )
    return jax.shard_map(
        shards,
        mesh=mesh,
        in_specs=placed,
        out_specs=(
            P(("gy", "gz"), "gx"),
            P(("gy", "gz"), "gx"),
            P("gx", ("gy", "gz")),
            P(("gy", "gz"), "gx"),
        ),
        check_vma=False,
    )
```

profile of v0, /device:TPU:0, one launch (start us, length us, event | category | flops | bytes accessed | tf_op | source)
XLA Modules:
  0.0 315.6 jit_solution(16967540374349955192)
XLA Ops:
  7.2 0.0 all-gather.3.cloned.1.call-start
  7.2 0.7 all-gather.3.cloned.1.call-update
  7.9 0.0 all-gather.5.cloned.1.call-start
  7.9 0.7 all-gather.5.cloned.1.call-update
  8.6 0.0 all-reduce.3.cloned.1.call-start
  8.7 26.3 %all-gather.3.cloned.1.call-done = bf16[192,3072]{1,0:T(8,128)(2,1)} async-done(((bf16[24,3072]{1,0:T(8,128)(2,1)}), bf16[192,3072]{1,0:T(8,128)(2,1)}) %all-gather.3.cloned.1.call-update) | async-done | bytes 1179664 | tf_op jit(solution)/shard_map/all_gather | solution.py:32
  35.0 12.0 %fusion.8 = f32[192,3072]{1,0:T(8,128)} fusion(bf16[192,3072]{1,0:T(8,128)(2,1)} %all-gather.3.cloned.1.call-done, bf16[3072,3072]{1,0:T(8,128)(2,1)} %param.6), kind=kOutput, calls=%fused_computation.13 | convolution fusion | flops 3623878656 | bytes 22413312 | tf_op jit(solution)/shard_map/dot_general | solution.py:35
  47.0 12.1 %all-gather.5.cloned.1.call-done = bf16[192,3072]{1,0:T(8,128)(2,1)} async-done(((bf16[24,3072]{1,0:T(8,128)(2,1)}), bf16[192,3072]{1,0:T(8,128)(2,1)}) %all-gather.5.cloned.1.call-update) | async-done | bytes 1179664 | tf_op jit(solution)/shard_map/all_gather | solution.py:33
  59.0 14.5 %fusion.9 = f32[192,3072]{1,0:T(8,128)} fusion(bf16[192,3072]{1,0:T(8,128)(2,1)} %all-gather.5.cloned.1.call-done, bf16[3072,3072]{1,0:T(8,128)(2,1)} %param.7), kind=kOutput, calls=%fused_computation.14 | convolution fusion | flops 3623878656 | bytes 22413312 | tf_op jit(solution)/shard_map/dot_general | solution.py:19
  73.5 0.0 all-reduce.3.cloned.1.call-update
  73.6 0.0 reduce-scatter.3.cloned.1.call-start
  73.6 112.7 %all-reduce.3.cloned.1.call-done = (f32[192,3072]{1,0:T(8,128)}, f32[192,3072]{1,0:T(8,128)}) async-done(((f32[192,3072]{1,0:T(8,128)}, f32[192,3072]{1,0:T(8,128)}), (f32[192,3072]{1,0:T(8,128)}, f32[192,3072]{1,0:T(8,128)})) %all-reduce.3.cloned.1.call-update) | async-done | bytes 4718608 | tf_op jit(solution)/shard_map/psum | solution.py:37
  186.3 12.6 %fusion.7 = f32[192,3072]{1,0:T(8,128)} fusion(bf16[3072,3072]{1,0:T(8,128)(2,1)} %param.7, f32[192,3072]{1,0:T(8,128)} %get-tuple-element.8), kind=kOutput, calls=%fused_computation.12 | convolution fusion | flops 3629187072 | bytes 23592960 | tf_op jit(solution)/shard_map/dot_general | solution.py:41
  198.9 0.0 reduce-scatter.3.cloned.1.call-update
  198.9 0.2 reduce-scatter.5.cloned.1.call-start
  199.2 1.4 copy-done
  200.6 3.1 fusion.6
  203.7 11.7 %fusion.10 = f32[192,3072]{1,0:T(8,128)} fusion(bf16[192,3072]{1,0:T(8,128)(2,1)S(1)} %fusion.6, bf16[3072,3072]{1,0:T(8,128)(2,1)} %param.6), kind=kOutput, calls=%fused_computation.15 | convolution fusion | flops 3623878656 | bytes 22413312 | tf_op jit(solution)/shard_map/dot_general | solution.py:19
  215.5 0.0 reduce-scatter.5.cloned.1.call-update
  215.5 10.8 %convert_bitcast_fusion = bf16[3072,3072]{0,1:T(8,128)(2,1)} fusion(bf16[192,3072]{1,0:T(8,128)(2,1)S(1)} %fusion.6, bf16[192,3072]{1,0:T(8,128)(2,1)} %all-gather.3.cloned.1.call-done), kind=kOutput, calls=%fused_computation | convolution fusion | flops 3633315840 | bytes 21233664 | tf_op jit(solution)/shard_map/dot_general | solution.py:25
  226.3 24.7 %copy.8 = bf16[3072,3072]{1,0:T(8,128)(2,1)} copy(bf16[3072,3072]{0,1:T(8,128)(2,1)} %convert_bitcast_fusion) | data formatting | bytes 37748736
  251.0 0.0 copy-done.1
  251.0 9.6 %convolution_convert_fusion = bf16[3072,3072]{1,0:T(8,128)(2,1)} fusion(bf16[192,3072]{1,0:T(8,128)(2,1)S(1)} %copy-done.1, f32[192,3072]{1,0:T(8,128)S(1)} %copy-done), kind=kOutput, calls=%fused_computation.1 | convolution fusion | flops 3638624256 | bytes 22413312 | tf_op jit(solution)/shard_map/dot_general | solution.py:25
  260.6 48.5 %reduce-scatter.5.cloned.1.call-done = f32[24,3072]{1,0:T(8,128)} async-done(((f32[192,3072]{1,0:T(8,128)}), f32[24,3072]{1,0:T(8,128)}) %reduce-scatter.5.cloned.1.call-update) | async-done | bytes 294928 | tf_op jit(solution)/shard_map/reduce_scatter | solution.py:47
  (3 shorter events, 0.0 us)
Async XLA Ops:
  7.2 27.8 %all-gather.3.cloned.1.call-start = ((), (), s32[]{:S(2)}) async-start(), calls=%async_computation.2 | async-start | bytes 1327104 | tf_op jit(solution)/shard_map/all_gather | solution.py:32
  7.9 51.1 %all-gather.5.cloned.1.call-start = ((), (), s32[]{:S(2)}) async-start(), calls=%async_computation.4 | async-start | bytes 1327104 | tf_op jit(solution)/shard_map/all_gather | solution.py:33
  8.6 177.7 %all-reduce.3.cloned.1.call-start = ((), (), s32[]{:S(2)}) async-start(), calls=%async_computation.6 | async-start | bytes 9437184 | tf_op jit(solution)/shard_map/psum | solution.py:37
  73.6 187.0 %reduce-scatter.3.cloned.1.call-start = ((), (), s32[]{:S(2)}) async-start(), calls=%async_computation.3 | async-start | bytes 2654208 | tf_op jit(solution)/shard_map/reduce_scatter | solution.py:40
  198.9 1.7 copy-start
  198.9 110.1 %reduce-scatter.5.cloned.1.call-start = ((), (), s32[]{:S(2)}) async-start(), calls=%async_computation.5 | async-start | bytes 2654208 | tf_op jit(solution)/shard_map/reduce_scatter | solution.py:47
  226.3 24.7 %copy-start.1 = (bf16[192,3072]{1,0:T(8,128)(2,1)S(1)}, bf16[192,3072]{1,0:T(8,128)(2,1)}, u32[]{:S(2)}) copy-start(bf16[192,3072]{1,0:T(8,128)(2,1)} %all-gather.5.cloned.1.call-done) | copy-start | bytes 3538948
Sparse Core Ops, SparseCore 0:
  9.6 25.3 all-gather.2
  36.6 22.4 all-gather.4
  73.7 112.6 all-reduce.2
  199.1 54.0 reduce-scatter.2
  255.9 53.1 reduce-scatter.4
where the time goes:
time: 316 us
  waiting for transfers between devices  201 us (64%)
  matrix products  71.1 us (22%)
  local copies, waits for them, and re-layouts  26.1 us (8%)
  between operations  13.8 us (4%)
    psum x1, waiting for transfers between devices, shards(): pre_sum, back_sum = lax.psum((pre_part, back_part), 'gx')  113 us
    reduce_scatter x1, waiting for transfers between devices, shards(): lax.psum_scatter(right_product(picked, w_in), ('gy', 'gz'), scatter_dimen...  48.5 us
    all_gather x1, waiting for transfers between devices, shards(): lax.all_gather(tokens, ('gy', 'gz'), axis=0, tiled=True)  26.3 us
    dot_general x2, matrix products, right_product(): lax.dot_general(left, right, (((1,), (1,)), ((), ())), preferred_element_...  26.2 us
    unnamed x5, local copies, waits for them, and re-layouts  26.1 us
    dot_general x2, matrix products, left_product(): lax.dot_general(left, right, (((0,), (0,)), ((), ())), preferred_element_...  20.4 us
    dot_general x1, matrix products, shards(): jnp.dot(picked, w_out, preferred_element_type=jnp.float32)  12.6 us
    all_gather x1, waiting for transfers between devices, shards(): lax.all_gather(grad_out, ('gy', 'gz'), axis=0, tiled=True)  12.1 us
  transfers between devices with their start and end apart: 5, of which 4 were waited for; matrix products, arithmetic and copies ran while one was open for 23% of the time, Pallas kernels for 0%

commit v1 on v0

--- a/solution.py
+++ b/solution.py
@@ -2,6 +2,26 @@
 import jax.numpy as jnp
 from jax import lax
 from jax.sharding import PartitionSpec as P
+
+
+def shape_members_all_by_axis(sample):
+    n_chips = lax.axis_size(("gy", "gz"))
+    all_blocks = [sample]
+    dev_j = 1
+    while dev_j < n_chips:
+        all_blocks.append(
+            lax.ppermute(
+                all_blocks[dev_j - 1],
+                ("gy", "gz"),
+                [(b, (b - 1) % n_chips) for b in range(n_chips)],
+            )
+        )
+        dev_j = dev_j + 1
+    return jnp.roll(
+        jnp.concatenate(all_blocks, axis=0),
+        shift=lax.axis_index(("gy", "gz")) * sample.shape[0],
+        axis=0,
+    )
 
 
 def activate(pre_sum, back_sum):
@@ -29,7 +49,7 @@
 
 def shards(tokens, grad_out, w_in, w_out):
     token_rows, grad_rows = (
-        lax.all_gather(tokens, ("gy", "gz"), axis=0, tiled=True),
+        shape_members_all_by_axis(tokens),
         lax.all_gather(grad_out, ("gy", "gz"), axis=0, tiled=True),
     )
     pre_part = jnp.dot(token_rows, w_in, preferred_element_type=jnp.float32)

time: 316 us -> 340 us (1.076)
  starting transfers between devices: 0.38 us -> 26.7 us
  local copies, waits for them, and re-layouts: 26.1 us -> 2.55 us
  waiting for transfers between devices: 201 us -> 224 us
    reduce_scatter x1, waiting for transfers between devices: 0.01 us -> 56 us  [shards(): lax.psum_scatter(jnp.dot(picked, w_out, preferred_element_type=jnp.float3...]
    ppermute x0 -> x7, waiting for transfers between devices: none -> 32.5 us  [shape_members_all_by_axis(): lax.ppermute(all_blocks[dev_j - 1], ('gy', 'gz'), [(b, (b - 1) % n_chips)...]
    reduce_scatter x1, waiting for transfers between devices: 48.5 us -> 19.9 us  [shards(): lax.psum_scatter(right_product(picked, w_in), ('gy', 'gz'), scatter_dimen...]
    ppermute x0 -> x7, starting transfers between devices: none -> 26.4 us  [shape_members_all_by_axis(): lax.ppermute(all_blocks[dev_j - 1], ('gy', 'gz'), [(b, (b - 1) % n_chips)...]
    all_gather x1 -> x0, waiting for transfers between devices: 26.3 us -> none  [shards(): lax.all_gather(tokens, ('gy', 'gz'), axis=0, tiled=True)]
    unnamed x5 -> x23, local copies, waits for them, and re-layouts: 26.1 us -> 2.53 us
    all_gather x1, waiting for transfers between devices: 12.1 us -> 0.01 us  [shards(): lax.all_gather(grad_out, ('gy', 'gz'), axis=0, tiled=True)]
  transfers between devices with their start and end apart: 5 -> 11, of which waited for: 4 -> 10; matrix products, arithmetic and copies ran while one was open for 23% -> 13% of each run, Pallas kernels for 0% -> 0%
where the time goes in v1:
time: 340 us
  waiting for transfers between devices  224 us (66%)
  matrix products  69.3 us (20%)
  starting transfers between devices  26.7 us (8%)
  between operations  13.9 us (4%)
  other arithmetic  3.86 us (1%)
    psum x1, waiting for transfers between devices, shards(): pre_sum, back_sum = lax.psum((pre_part, back_part), 'gx')  115 us
    reduce_scatter x1, waiting for transfers between devices, shards(): lax.psum_scatter(jnp.dot(picked, w_out, preferred_element_type=jnp.float3...  56 us
    ppermute x7, waiting for transfers between devices, shape_members_all_by_axis(): lax.ppermute(all_blocks[dev_j - 1], ('gy', 'gz'), [(b, (b - 1) % n_chips)...  32.5 us
    ppermute x7, starting transfers between devices, shape_members_all_by_axis(): lax.ppermute(all_blocks[dev_j - 1], ('gy', 'gz'), [(b, (b - 1) % n_chips)...  26.4 us
    dot_general x2, matrix products, right_product(): lax.dot_general(left, right, (((1,), (1,)), ((), ())), preferred_element_...  26 us
    dot_general x2, matrix products, left_product(): lax.dot_general(left, right, (((0,), (0,)), ((), ())), preferred_element_...  20.5 us
    reduce_scatter x1, waiting for transfers between devices, shards(): lax.psum_scatter(right_product(picked, w_in), ('gy', 'gz'), scatter_dimen...  19.9 us
    dot_general x1, matrix products, shards(): jnp.dot(picked, w_out, preferred_element_type=jnp.float32)  12.1 us
  transfers between devices with their start and end apart: 11, of which 10 were waited for; matrix products, arithmetic and copies ran while one was open for 13% of the time, Pallas kernels for 0%

profile of v1, /device:TPU:0, one launch (start us, length us, event | category | flops | bytes accessed | tf_op | source)
XLA Modules:
  0.0 340.1 jit_solution(4537127508412714284)
XLA Ops:
  8.0 4.5 %collective-permute-start = (bf16[24,3072]{1,0:T(8,128)(2,1)}, bf16[24,3072]{1,0:T(8,128)(2,1)S(1)}, u32[]{:S(2)}, u32[]{:S(2)}) collective-permute-start(bf16[24,3072]{1,0:T(8,128)(2,1)} %param.4), channel_id=1, source_target_pairs={{0,7},{1,0},{2,1},{3,2},{4,3},{5,4},{6,5},{7,6},{8,15},{9,8},{10,9... | collective-permute-start | bytes 442376 | tf_op jit(solution)/shard_map/ppermute | solution.py:13
  13.5 3.6 %collective-permute-done = bf16[24,3072]{1,0:T(8,128)(2,1)S(1)} collective-permute-done((bf16[24,3072]{1,0:T(8,128)(2,1)}, bf16[24,3072]{1,0:T(8,128)(2,1)S(1)}, u32[]{:S(2)}, u32[]{:S(2)}) %collective-permute-start) | collective-permute-done | bytes 147488 | tf_op jit(solution)/shard_map/ppermute | solution.py:13
  17.0 3.9 %collective-permute-start.1 = (bf16[24,3072]{1,0:T(8,128)(2,1)S(1)}, bf16[24,3072]{1,0:T(8,128)(2,1)S(1)}, u32[]{:S(2)}, u32[]{:S(2)}) collective-permute-start(bf16[24,3072]{1,0:T(8,128)(2,1)S(1)} %collective-permute-done), channel_id=1, source_target_pairs={{0,7},{1,0},{2,1},{3,2},{4,3},{5,4},{6,5},{7,6},{8,15},{9,8},{10,9... | collective-permute-start | bytes 442376 | tf_op jit(solution)/shard_map/ppermute | solution.py:13
  20.9 7.2 %collective-permute-done.1 = bf16[24,3072]{1,0:T(8,128)(2,1)S(1)} collective-permute-done((bf16[24,3072]{1,0:T(8,128)(2,1)S(1)}, bf16[24,3072]{1,0:T(8,128)(2,1)S(1)}, u32[]{:S(2)}, u32[]{:S(2)}) %collective-permute-start.1) | collective-permute-done | bytes 147488 | tf_op jit(solution)/shard_map/ppermute | solution.py:13
  28.1 3.7 %collective-permute-start.2 = (bf16[24,3072]{1,0:T(8,128)(2,1)S(1)}, bf16[24,3072]{1,0:T(8,128)(2,1)S(1)}, u32[]{:S(2)}, u32[]{:S(2)}) collective-permute-start(bf16[24,3072]{1,0:T(8,128)(2,1)S(1)} %collective-permute-done.1), channel_id=1, source_target_pairs={{0,7},{1,0},{2,1},{3,2},{4,3},{5,4},{6,5},{7,6},{8,15},{9,8},{10,9... | collective-permute-start | bytes 442376 | tf_op jit(solution)/shard_map/ppermute | solution.py:13
  31.9 6.0 %collective-permute-done.2 = bf16[24,3072]{1,0:T(8,128)(2,1)S(1)} collective-permute-done((bf16[24,3072]{1,0:T(8,128)(2,1)S(1)}, bf16[24,3072]{1,0:T(8,128)(2,1)S(1)}, u32[]{:S(2)}, u32[]{:S(2)}) %collective-permute-start.2) | collective-permute-done | bytes 147488 | tf_op jit(solution)/shard_map/ppermute | solution.py:13
  37.9 3.1 collective-permute-start.3
  41.0 3.9 %collective-permute-done.3 = bf16[24,3072]{1,0:T(8,128)(2,1)S(1)} collective-permute-done((bf16[24,3072]{1,0:T(8,128)(2,1)S(1)}, bf16[24,3072]{1,0:T(8,128)(2,1)S(1)}, u32[]{:S(2)}, u32[]{:S(2)}) %collective-permute-start.3) | collective-permute-done | bytes 147488 | tf_op jit(solution)/shard_map/ppermute | solution.py:13
  44.9 3.7 %collective-permute-start.4 = (bf16[24,3072]{1,0:T(8,128)(2,1)S(1)}, bf16[24,3072]{1,0:T(8,128)(2,1)S(1)}, u32[]{:S(2)}, u32[]{:S(2)}) collective-permute-start(bf16[24,3072]{1,0:T(8,128)(2,1)S(1)} %collective-permute-done.3), channel_id=1, source_target_pairs={{0,7},{1,0},{2,1},{3,2},{4,3},{5,4},{6,5},{7,6},{8,15},{9,8},{10,9... | collective-permute-start | bytes 442376 | tf_op jit(solution)/shard_map/ppermute | solution.py:13
  48.6 3.9 %collective-permute-done.4 = bf16[24,3072]{1,0:T(8,128)(2,1)S(1)} collective-permute-done((bf16[24,3072]{1,0:T(8,128)(2,1)S(1)}, bf16[24,3072]{1,0:T(8,128)(2,1)S(1)}, u32[]{:S(2)}, u32[]{:S(2)}) %collective-permute-start.4) | collective-permute-done | bytes 147488 | tf_op jit(solution)/shard_map/ppermute | solution.py:13
  52.6 3.7 %collective-permute-start.5 = (bf16[24,3072]{1,0:T(8,128)(2,1)S(1)}, bf16[24,3072]{1,0:T(8,128)(2,1)S(1)}, u32[]{:S(2)}, u32[]{:S(2)}) collective-permute-start(bf16[24,3072]{1,0:T(8,128)(2,1)S(1)} %collective-permute-done.4), channel_id=1, source_target_pairs={{0,7},{1,0},{2,1},{3,2},{4,3},{5,4},{6,5},{7,6},{8,15},{9,8},{10,9... | collective-permute-start | bytes 442376 | tf_op jit(solution)/shard_map/ppermute | solution.py:13
  56.3 3.9 %collective-permute-done.5 = bf16[24,3072]{1,0:T(8,128)(2,1)S(1)} collective-permute-done((bf16[24,3072]{1,0:T(8,128)(2,1)S(1)}, bf16[24,3072]{1,0:T(8,128)(2,1)S(1)}, u32[]{:S(2)}, u32[]{:S(2)}) %collective-permute-start.5) | collective-permute-done | bytes 147488 | tf_op jit(solution)/shard_map/ppermute | solution.py:13
  60.2 3.7 %collective-permute-start.6 = (bf16[24,3072]{1,0:T(8,128)(2,1)S(1)}, bf16[24,3072]{1,0:T(8,128)(2,1)S(1)}, u32[]{:S(2)}, u32[]{:S(2)}) collective-permute-start(bf16[24,3072]{1,0:T(8,128)(2,1)S(1)} %collective-permute-done.5), channel_id=1, source_target_pairs={{0,7},{1,0},{2,1},{3,2},{4,3},{5,4},{6,5},{7,6},{8,15},{9,8},{10,9... | collective-permute-start | bytes 442376 | tf_op jit(solution)/shard_map/ppermute | solution.py:13
  63.9 3.9 %collective-permute-done.6 = bf16[24,3072]{1,0:T(8,128)(2,1)S(1)} collective-permute-done((bf16[24,3072]{1,0:T(8,128)(2,1)S(1)}, bf16[24,3072]{1,0:T(8,128)(2,1)S(1)}, u32[]{:S(2)}, u32[]{:S(2)}) %collective-permute-start.6) | collective-permute-done | bytes 147488 | tf_op jit(solution)/shard_map/ppermute | solution.py:13
  68.1 10.7 %fusion.8 = f32[192,3072]{1,0:T(8,128)} fusion(bf16[3072,3072]{1,0:T(8,128)(2,1)} %param.6, bf16[384,3072]{1,0:T(8,128)(2,1)S(1)} %constant_dynamic-update-slice_fusion, s32[]{:T(128)S(6)} %select_n.14), kind=kOutput, calls=%fused_computation.13 | convolution fusion | flops 3623878656 | bytes 22413316 | tf_op jit(solution)/shard_map/dot_general | solution.py:55
  78.7 14.5 %fusion.13 = f32[192,3072]{1,0:T(8,128)} fusion(bf16[192,3072]{1,0:T(8,128)(2,1)} %all-gather.2.cloned.1.call-done, bf16[3072,3072]{1,0:T(8,128)(2,1)} %param.7), kind=kOutput, calls=%fused_computation.34 | convolution fusion | flops 3623878656 | bytes 22413312 | tf_op jit(solution)/shard_map/dot_general | solution.py:39
  93.3 114.7 %all-reduce.3.cloned.1.call-done = (f32[192,3072]{1,0:T(8,128)}, f32[192,3072]{1,0:T(8,128)}) async-done(((f32[192,3072]{1,0:T(8,128)}, f32[192,3072]{1,0:T(8,128)}), (f32[192,3072]{1,0:T(8,128)}, f32[192,3072]{1,0:T(8,128)})) %all-reduce.3.cloned.1.call-update) | async-done | bytes 4718608 | tf_op jit(solution)/shard_map/psum | solution.py:57
  208.0 3.9 %fusion.6 = bf16[192,3072]{1,0:T(8,128)(2,1)S(1)} fusion(f32[192,3072]{1,0:T(8,128)} %get-tuple-element.5, f32[192,3072]{1,0:T(8,128)} %get-tuple-element.4), kind=kLoop, calls=%fused_computation.10 | loop fusion | flops 11206656 | bytes 5898240 | tf_op jit(solution)/shard_map/convert_element_type | solution.py:35
  211.9 11.5 %fusion.14 = f32[192,3072]{1,0:T(8,128)} fusion(bf16[192,3072]{1,0:T(8,128)(2,1)S(1)} %fusion.6, bf16[3072,3072]{1,0:T(8,128)(2,1)} %param.6), kind=kOutput, calls=%fused_computation.35 | convolution fusion | flops 3623878656 | bytes 22413312 | tf_op jit(solution)/shard_map/dot_general | solution.py:39
  225.1 12.1 %fusion.12 = f32[192,3072]{1,0:T(8,128)} fusion(bf16[3072,3072]{1,0:T(8,128)(2,1)} %param.7, f32[192,3072]{1,0:T(8,128)S(1)} %copy-done), kind=kOutput, calls=%fused_computation.33 | convolution fusion | flops 3629187072 | bytes 23592960 | tf_op jit(solution)/shard_map/dot_general | solution.py:61
  237.2 10.9 %convolution_convert_fusion.1 = bf16[3072,3072]{1,0:T(8,128)(2,1)} fusion(bf16[192,3072]{1,0:T(8,128)(2,1)S(1)} %fusion.6, bf16[384,3072]{1,0:T(8,128)(2,1)} %copy-done.2, s32[]{:T(128)S(6)} %select_n.14), kind=kOutput, calls=%fused_computation.1 | convolution fusion | flops 3633315840 | bytes 21233668 | tf_op jit(solution)/shard_map/dot_general | solution.py:45
  248.2 9.6 %convolution_convert_fusion = bf16[3072,3072]{1,0:T(8,128)(2,1)} fusion(bf16[192,3072]{1,0:T(8,128)(2,1)S(1)} %copy-done.1, f32[192,3072]{1,0:T(8,128)S(1)} %copy-done), kind=kOutput, calls=%fused_computation | convolution fusion | flops 3638624256 | bytes 22413312 | tf_op jit(solution)/shard_map/dot_general | solution.py:45
  257.7 19.9 %reduce-scatter.5.cloned.1.call-done = f32[24,3072]{1,0:T(8,128)} async-done(((f32[192,3072]{1,0:T(8,128)}), f32[24,3072]{1,0:T(8,128)}) %reduce-scatter.5.cloned.1.call-update) | async-done | bytes 294928 | tf_op jit(solution)/shard_map/reduce_scatter | solution.py:67
  277.6 56.0 %reduce-scatter.3.cloned.1.call-done = f32[24,3072]{1,0:T(8,128)} async-done(((f32[192,3072]{1,0:T(8,128)}), f32[24,3072]{1,0:T(8,128)}) %reduce-scatter.3.cloned.1.call-update) | async-done | bytes 294928 | tf_op jit(solution)/shard_map/reduce_scatter | solution.py:60
  (33 shorter events, 3.6 us)
Async XLA Ops:
  7.2 60.7 %copy-start.3 = (bf16[24,3072]{1,0:T(8,128)(2,1)S(1)}, bf16[24,3072]{1,0:T(8,128)(2,1)}, u32[]{:S(2)}) copy-start(bf16[24,3072]{1,0:T(8,128)(2,1)} %param.4) | copy-start | bytes 442372
  7.2 71.6 %all-gather.2.cloned.1.call-start = ((), (), s32[]{:S(2)}) async-start(), calls=%async_computation.3 | async-start | bytes 1327104 | tf_op jit(solution)/shard_map/all_gather | solution.py:53
  7.9 200.1 %all-reduce.3.cloned.1.call-start = ((), (), s32[]{:S(2)}) async-start(), calls=%async_computation.5 | async-start | bytes 9437184 | tf_op jit(solution)/shard_map/psum | solution.py:57
  8.0 9.1 %collective-permute-start = (bf16[24,3072]{1,0:T(8,128)(2,1)}, bf16[24,3072]{1,0:T(8,128)(2,1)S(1)}, u32[]{:S(2)}, u32[]{:S(2)}) collective-permute-start(bf16[24,3072]{1,0:T(8,128)(2,1)} %param.4), channel_id=1, source_target_pairs={{0,7},{1,0},{2,1},{3,2},{4,3},{5,4},{6,5},{7,6},{8,15},{9,8},{10,9... | collective-permute-start | bytes 442376 | tf_op jit(solution)/shard_map/ppermute | solution.py:13
  17.0 11.1 %collective-permute-start.1 = (bf16[24,3072]{1,0:T(8,128)(2,1)S(1)}, bf16[24,3072]{1,0:T(8,128)(2,1)S(1)}, u32[]{:S(2)}, u32[]{:S(2)}) collective-permute-start(bf16[24,3072]{1,0:T(8,128)(2,1)S(1)} %collective-permute-done), channel_id=1, source_target_pairs={{0,7},{1,0},{2,1},{3,2},{4,3},{5,4},{6,5},{7,6},{8,15},{9,8},{10,9... | collective-permute-start | bytes 442376 | tf_op jit(solution)/shard_map/ppermute | solution.py:13
  28.1 9.8 %collective-permute-start.2 = (bf16[24,3072]{1,0:T(8,128)(2,1)S(1)}, bf16[24,3072]{1,0:T(8,128)(2,1)S(1)}, u32[]{:S(2)}, u32[]{:S(2)}) collective-permute-start(bf16[24,3072]{1,0:T(8,128)(2,1)S(1)} %collective-permute-done.1), channel_id=1, source_target_pairs={{0,7},{1,0},{2,1},{3,2},{4,3},{5,4},{6,5},{7,6},{8,15},{9,8},{10,9... | collective-permute-start | bytes 442376 | tf_op jit(solution)/shard_map/ppermute | solution.py:13
  37.9 7.0 %collective-permute-start.3 = (bf16[24,3072]{1,0:T(8,128)(2,1)S(1)}, bf16[24,3072]{1,0:T(8,128)(2,1)S(1)}, u32[]{:S(2)}, u32[]{:S(2)}) collective-permute-start(bf16[24,3072]{1,0:T(8,128)(2,1)S(1)} %collective-permute-done.2), channel_id=1, source_target_pairs={{0,7},{1,0},{2,1},{3,2},{4,3},{5,4},{6,5},{7,6},{8,15},{9,8},{10,9... | collective-permute-start | bytes 442376 | tf_op jit(solution)/shard_map/ppermute | solution.py:13
  44.9 7.7 %collective-permute-start.4 = (bf16[24,3072]{1,0:T(8,128)(2,1)S(1)}, bf16[24,3072]{1,0:T(8,128)(2,1)S(1)}, u32[]{:S(2)}, u32[]{:S(2)}) collective-permute-start(bf16[24,3072]{1,0:T(8,128)(2,1)S(1)} %collective-permute-done.3), channel_id=1, source_target_pairs={{0,7},{1,0},{2,1},{3,2},{4,3},{5,4},{6,5},{7,6},{8,15},{9,8},{10,9... | collective-permute-start | bytes 442376 | tf_op jit(solution)/shard_map/ppermute | solution.py:13
  52.6 7.7 %collective-permute-start.5 = (bf16[24,3072]{1,0:T(8,128)(2,1)S(1)}, bf16[24,3072]{1,0:T(8,128)(2,1)S(1)}, u32[]{:S(2)}, u32[]{:S(2)}) collective-permute-start(bf16[24,3072]{1,0:T(8,128)(2,1)S(1)} %collective-permute-done.4), channel_id=1, source_target_pairs={{0,7},{1,0},{2,1},{3,2},{4,3},{5,4},{6,5},{7,6},{8,15},{9,8},{10,9... | collective-permute-start | bytes 442376 | tf_op jit(solution)/shard_map/ppermute | solution.py:13
  60.2 7.7 %collective-permute-start.6 = (bf16[24,3072]{1,0:T(8,128)(2,1)S(1)}, bf16[24,3072]{1,0:T(8,128)(2,1)S(1)}, u32[]{:S(2)}, u32[]{:S(2)}) collective-permute-start(bf16[24,3072]{1,0:T(8,128)(2,1)S(1)} %collective-permute-done.5), channel_id=1, source_target_pairs={{0,7},{1,0},{2,1},{3,2},{4,3},{5,4},{6,5},{7,6},{8,15},{9,8},{10,9... | collective-permute-start | bytes 442376 | tf_op jit(solution)/shard_map/ppermute | solution.py:13
  68.0 10.7 %copy-start.2 = (bf16[384,3072]{1,0:T(8,128)(2,1)}, bf16[384,3072]{1,0:T(8,128)(2,1)S(1)}, u32[]{:S(2)}) copy-start(bf16[384,3072]{1,0:T(8,128)(2,1)S(1)} %constant_dynamic-update-slice_fusion) | copy-start | bytes 7077892
  93.2 184.4 %reduce-scatter.5.cloned.1.call-start = ((), (), s32[]{:S(2)}) async-start(), calls=%async_computation.4 | async-start | bytes 2654208 | tf_op jit(solution)/shard_map/reduce_scatter | solution.py:67
  223.4 1.7 copy-start
  223.5 110.1 %reduce-scatter.3.cloned.1.call-start = ((), (), s32[]{:S(2)}) async-start(), calls=%async_computation.2 | async-start | bytes 2654208 | tf_op jit(solution)/shard_map/reduce_scatter | solution.py:60
  237.2 10.9 %copy-start.1 = (bf16[192,3072]{1,0:T(8,128)(2,1)S(1)}, bf16[192,3072]{1,0:T(8,128)(2,1)}, u32[]{:S(2)}) copy-start(bf16[192,3072]{1,0:T(8,128)(2,1)} %all-gather.2.cloned.1.call-done) | copy-start | bytes 3538948
Sparse Core Ops, SparseCore 0:
  9.6 28.5 all-gather.1
  93.4 114.6 all-reduce.2
  223.6 54.0 reduce-scatter.4
  280.4 53.1 reduce-scatter.2
